TPU v7x, 32 devices: a whole 2x2x4 slice. The times are simulated.
32 devices in a mesh: rows: 8 (over z, y), cols: 4 (over x, core).
Axes of the slice: x: 2, y: 2, z: 4, core: 2. Of those that a mesh axis runs over, the one named last changes fastest.
Arguments:
- sketch: float32 [32768, 256], P(('rows', 'cols'))
- tiles: bfloat16 [1280, 512, 512], P(('rows', 'cols')), may hold values from -48 to 48
- tile_user: int32 [1280], P(('rows', 'cols')), may hold values from 0 to 7
- tile_item: int32 [1280], P(('rows', 'cols')), may hold values from 0 to 7
- tile_count: int32 [32], P(('rows', 'cols')), may hold values from 5 to 40, as said below
- item_owner: int32 [4, 8], P('cols'), may hold values from 0 to 7, each once within a row
Outputs:
- projected: float32 [8, 4, 256, 512], P('rows', 'cols')
Inputs may be any that keep to these rules, and one draw needn't show every extreme that they name: `tile_count`: live slots of a device are its first slots; some device has all 40 live in every draw.
All inputs are finite; a program needn't handle non-finite values.
Results may differ from a plain program's by a relative error of at most 0.0029.
Values may be sent and summed in bfloat16 or wider, within the bound.
No kernel may reach another device: no remote copies, remote signals or barrier semaphores. Data moves between devices by JAX's collectives and lax.ppermute only.
A program may use at most 192 MiB of HBM per device.

v0:
```python
import jax
import jax.numpy as jnp
from jax import lax
from jax.sharding import PartitionSpec as P


def accumulate(totals, tile_set, users, items, owner, slab, stop, first_row):
    tile_size = tile_set.shape[1]
    row_count = totals.shape[0]

    def step(index, partial_sums):
        target = owner[items[index]] - first_row
        inside = jnp.logical_and(target >= 0, target < row_count)

        def add_tile(sums):
            basis_rows = lax.dynamic_slice_in_dim(slab, users[index] * tile_size, tile_size, 0)
            partial_value = lax.dot_general(
                basis_rows,
                tile_set[index],
                (((0,), (0,)), ((), ())),
                preferred_element_type=jnp.float32,
            )
            place = jnp.clip(target, 0, row_count - 1)
            current = lax.dynamic_index_in_dim(sums, place, 0, keepdims=False)
            return lax.dynamic_update_index_in_dim(sums, current + partial_value, place, 0)

        return lax.cond(inside, add_tile, lambda sums: sums, partial_sums)

    return lax.fori_loop(0, stop, step, totals)


def body(sketch, tiles, tile_user, tile_item, tile_count, item_owner):
    gram = lax.dot_general(
        sketch,
        sketch,
        (((0,), (0,)), ((), ())),
        precision=lax.Precision.HIGHEST,
        preferred_element_type=jnp.float32,
    )
    total = lax.psum(gram, ("rows", "cols"))
    lower_factor = jnp.linalg.cholesky(total)
    basis_full = lax.linalg.triangular_solve(
        lower_factor, sketch, left_side=False, lower=True, transpose_a=True
    )
    basis = basis_full.astype(jnp.bfloat16)
    slab = lax.all_gather(basis, "cols", axis=0, tiled=True)
    owner = item_owner[0]
    live_count = tile_count[0]
    width = sketch.shape[1]
    tile_size = tiles.shape[2]
    totals = jnp.zeros((owner.shape[0], width, tile_size), jnp.float32)
    totals = accumulate(totals, tiles, tile_user, tile_item, owner, slab, live_count, 0)
    owned = lax.psum_scatter(totals, "rows", scatter_dimension=0, tiled=True)
    return owned[:, None]


def solution(mesh):
    placed = (
        P(("rows", "cols"), None),
        P(("rows", "cols"), None, None),
        P(("rows", "cols")),
        P(("rows", "cols")),
        P(("rows", "cols")),
        P("cols", None),
    )
    return jax.shard_map(
        body, mesh=mesh, in_specs=placed, out_specs=P("rows", "cols", None, None), check_vma=False
    )
```

profile of v0, /device:TPU:0, one launch (start us, length us, event | category | flops | bytes accessed | tf_op | source)
XLA Modules:
  0.0 737.1 jit_solution(1801150780538099880)
XLA Ops:
  6.5 4.1 fusion.14
  10.8 129.7 %all-reduce.3.cloned.1.call-done = f32[256,256]{0,1:T(8,128)} async-done(((f32[256,256]{0,1:T(8,128)}), f32[256,256]{0,1:T(8,128)}) %all-reduce.3.cloned.1.call-update) | async-done | bytes 262160 | tf_op jit(solution)/shard_map/psum | solution.py:40
  142.6 11.7 %cholesky.50 = f32[128,128]{1,0:T(8,128)S(1)} custom-call(f32[128,128]{1,0:T(8,128)S(1)} %cholesky.118), custom_call_target="Cholesky" | custom-call | tf_op jit(solution)/shard_map/jit(cholesky)/cholesky | solution.py:41
  154.3 9.8 %custom-call.14 = f32[1,128,128]{1,2,0:T(8,128)S(1)} custom-call(f32[1,128,128]{2,1,0:T(8,128)S(1)} %get-tuple-element.116), custom_call_target="InvertDiagBlocksLowerTriangular" | custom-call | tf_op jit(solution)/shard_map/jit(cholesky)/cholesky | solution.py:41
  164.7 11.7 %cholesky.105 = f32[128,128]{1,0:T(8,128)S(1)} custom-call(f32[128,128]{1,0:T(8,128)S(1)} %convolution_subtract_fusion.1), custom_call_target="Cholesky" | custom-call | tf_op jit(solution)/shard_map/jit(cholesky)/cholesky | solution.py:41
  178.4 4.1 while.15
  179.2 1.4 bitcast_dynamic-update-slice_fusion.2
  181.1 1.4 bitcast_dynamic-update-slice_fusion.2
  182.5 19.7 %custom-call.15 = f32[2,128,128]{1,2,0:T(8,128)S(1)} custom-call(f32[2,128,128]{2,1,0:T(8,128)S(1)} %get-tuple-element.78), custom_call_target="InvertDiagBlocksLowerTriangular" | custom-call | tf_op jit(solution)/shard_map/triangular_solve | solution.py:42
  205.5 21.7 %all-gather.2.cloned.1.call-done = bf16[4096,256]{0,1:T(8,128)(2,1)} async-done(((bf16[1024,256]{0,1:T(8,128)(2,1)}), bf16[4096,256]{0,1:T(8,128)(2,1)}) %all-gather.2.cloned.1.call-update) | async-done | bytes 2097168 | tf_op jit(solution)/shard_map/all_gather | solution.py:46
  227.1 3.3 copy.9
  230.4 2.5 broadcast_in_dim.12
  232.9 51.8 %while.14 = (s32[]{:T(128)}, f32[8,256,512]{2,1,0:T(8,128)}, s32[]{:T(128)}, s32[40]{0:T(128)S(1)}, s32[8]{0:T(128)S(1)}, /*index=5*/s32[40]{0:T(128)S(1)}, bf16...) while((s32[]{:T(128)}, f32[8,256,512]{2,1,0:T(8,128)}, ...), condition=%wide.region_8.9_spmd, body=%wide.region_5.8_spmd.sunk | while | flops 134348832 | bytes 2884007 | solution.py:29
  238.0 5.1 conditional.2
  241.0 2.2 fusion.1
  248.2 5.1 conditional.2
  251.2 2.2 fusion.1
  258.4 5.1 conditional.2
  261.4 2.2 fusion.1
  268.7 5.2 conditional.2
  271.6 2.2 fusion.1
  278.9 5.2 conditional.2
  281.9 2.2 fusion.1
  284.7 445.8 %reduce-scatter.2.cloned.1.call-done = f32[1,256,512]{2,1,0:T(8,128)} async-done(((f32[8,256,512]{2,1,0:T(8,128)}), f32[1,256,512]{2,1,0:T(8,128)}) %reduce-scatter.2.cloned.1.call-update) | async-done | bytes 524304 | tf_op jit(solution)/shard_map/reduce_scatter | solution.py:53
  (56 shorter events, 22.1 us)
Async XLA Ops:
  6.5 195.7 %copy-start = (f32[1024,256]{1,0:T(8,128)S(1)}, f32[1024,256]{1,0:T(8,128)}, u32[]{:S(2)}) copy-start(f32[1024,256]{1,0:T(8,128)} %param.10) | copy-start | bytes 3145732
  6.5 134.0 %all-reduce.3.cloned.1.call-start = ((), (), s32[]{:S(2)}) async-start(), calls=%async_computation.1 | async-start | bytes 524288 | tf_op jit(solution)/shard_map/psum | solution.py:40
  10.7 216.4 %all-gather.2.cloned.1.call-start = ((), (), s32[]{:S(2)}) async-start(), calls=%async_computation.2 | async-start | bytes 2621440 | tf_op jit(solution)/shard_map/all_gather | solution.py:46
  205.4 525.2 %reduce-scatter.2.cloned.1.call-start = ((), (), s32[]{:S(2)}) async-start(), calls=%async_computation.3 | async-start | bytes 4718592 | tf_op jit(solution)/shard_map/reduce_scatter | solution.py:53
  205.4 27.5 %copy-start.1 = (s32[40]{0:T(128)S(1)}, s32[40]{0:T(128)}, u32[]{:S(2)}) copy-start(s32[40]{0:T(128)} %param.13) | copy-start | bytes 484
  205.4 27.5 %copy-start.2 = (s32[1,8]{1,0:T(1,128)S(1)}, s32[1,8]{1,0:T(1,128)}, u32[]{:S(2)}) copy-start(s32[1,8]{1,0:T(1,128)} %param.15) | copy-start | bytes 100
  205.5 27.4 %copy-start.3 = (s32[40]{0:T(128)S(1)}, s32[40]{0:T(128)}, u32[]{:S(2)}) copy-start(s32[40]{0:T(128)} %param.12) | copy-start | bytes 484
Sparse Core Ops, SparseCore 0:
  12.9 127.5 all-reduce.2
  205.5 21.5 all-gather.1
  284.9 445.6 reduce-scatter.1
where the time goes:
time: 744 us; the launch traced here: 737 us
  waiting for transfers between devices  597 us (80%)
  other arithmetic  55.5 us (7%)
  loops' own time  26.9 us (4%)
  local copies, waits for them, and re-layouts  25.1 us (3%)
  matrix products  17.7 us (2%)
  between operations  14.5 us (2%)
    reduce_scatter x1, waiting for transfers between devices, body(): owned = lax.psum_scatter(totals, 'rows', scatter_dimension=0, tiled=True)  446 us
    psum x1, waiting for transfers between devices, body(): total = lax.psum(gram, ('rows', 'cols'))  130 us
    another operation x6, other arithmetic, body(): lower_factor = jnp.linalg.cholesky(total)  34 us
    all_gather x1, waiting for transfers between devices, body(): slab = lax.all_gather(basis, 'cols', axis=0, tiled=True)  21.7 us
    another operation x5, other arithmetic, body(): lax.linalg.triangular_solve(lower_factor, sketch, left_side=False, lower=...  20.6 us
    another operation x1, loops' own time, accumulate(): return lax.fori_loop(0, stop, step, totals)  20.2 us
  transfers between devices with their start and end apart: 3, of which 3 were waited for; matrix products, arithmetic and copies ran while one was open for 0% of the time, Pallas kernels for 0%

commit v1 on v0

--- a/solution.py
+++ b/solution.py
@@ -37,7 +37,7 @@
         precision=lax.Precision.HIGHEST,
         preferred_element_type=jnp.float32,
     )
-    total = lax.psum(gram, ("rows", "cols"))
+    total = jnp.sum(lax.all_gather(gram, ("rows", "cols")), axis=0)
     lower_factor = jnp.linalg.cholesky(total)
     basis_full = lax.linalg.triangular_solve(
         lower_factor, sketch, left_side=False, lower=True, transpose_a=True

time: 744 us -> 696 us (0.935)
  waiting for transfers between devices: 597 us -> 547 us
    psum x1 -> x0, waiting for transfers between devices: 130 us -> none  [body(): total = lax.psum(gram, ('rows', 'cols'))]
    all_gather x0 -> x1, waiting for transfers between devices: none -> 80.2 us  [body(): total = jnp.sum(lax.all_gather(gram, ('rows', 'cols')), axis=0)]
where the time goes in v1:
time: 696 us; the launch traced here: 689 us
  waiting for transfers between devices  547 us (79%)
  other arithmetic  58.6 us (8%)
  loops' own time  26.9 us (4%)
  local copies, waits for them, and re-layouts  24.1 us (3%)
  matrix products  17.7 us (3%)
  between operations  14.5 us (2%)
    reduce_scatter x1, waiting for transfers between devices, body(): owned = lax.psum_scatter(totals, 'rows', scatter_dimension=0, tiled=True)  446 us
    all_gather x1, waiting for transfers between devices, body(): total = jnp.sum(lax.all_gather(gram, ('rows', 'cols')), axis=0)  80.2 us
    another operation x6, other arithmetic, body(): lower_factor = jnp.linalg.cholesky(total)  34 us
    all_gather x1, waiting for transfers between devices, body(): slab = lax.all_gather(basis, 'cols', axis=0, tiled=True)  21.2 us
    another operation x5, other arithmetic, body(): lax.linalg.triangular_solve(lower_factor, sketch, left_side=False, lower=...  20.6 us
    another operation x1, loops' own time, accumulate(): return lax.fori_loop(0, stop, step, totals)  20.2 us
  transfers between devices with their start and end apart: 3, of which 3 were waited for; matrix products, arithmetic and copies ran while one was open for 0% of the time, Pallas kernels for 0%

profile of v1, /device:TPU:0, one launch (start us, length us, event | category | flops | bytes accessed | tf_op | source)
XLA Modules:
  0.0 689.2 jit_solution(13729971890113179211)
XLA Ops:
  6.5 4.1 fusion.14
  10.7 80.2 %all-gather.6.cloned.1.call-done = f32[8192,256]{1,0:T(8,128)} async-done(((f32[256,256]{1,0:T(8,128)}), f32[8192,256]{1,0:T(8,128)}) %all-gather.6.cloned.1.call-update) | async-done | bytes 8388624 | tf_op jit(solution)/shard_map/all_gather | solution.py:40
  90.9 4.0 reduce_sum.9
  95.1 11.7 %cholesky.50 = f32[128,128]{1,0:T(8,128)S(1)} custom-call(f32[128,128]{1,0:T(8,128)S(1)} %cholesky.118), custom_call_target="Cholesky" | custom-call | tf_op jit(solution)/shard_map/jit(cholesky)/cholesky | solution.py:41
  106.9 9.8 %custom-call.14 = f32[1,128,128]{1,2,0:T(8,128)S(1)} custom-call(f32[1,128,128]{2,1,0:T(8,128)S(1)} %get-tuple-element.124), custom_call_target="InvertDiagBlocksLowerTriangular" | custom-call | tf_op jit(solution)/shard_map/jit(cholesky)/cholesky | solution.py:41
  117.2 11.7 %cholesky.105 = f32[128,128]{1,0:T(8,128)S(1)} custom-call(f32[128,128]{1,0:T(8,128)S(1)} %convolution_subtract_fusion.1), custom_call_target="Cholesky" | custom-call | tf_op jit(solution)/shard_map/jit(cholesky)/cholesky | solution.py:41
  131.0 4.1 while.15
  131.7 1.4 bitcast_dynamic-update-slice_fusion.2
  135.1 19.7 %custom-call.15 = f32[2,128,128]{1,2,0:T(8,128)S(1)} custom-call(f32[2,128,128]{2,1,0:T(8,128)S(1)} %get-tuple-element.78), custom_call_target="InvertDiagBlocksLowerTriangular" | custom-call | tf_op jit(solution)/shard_map/triangular_solve | solution.py:42
  158.0 21.2 %all-gather.4.cloned.1.call-done = bf16[4096,256]{0,1:T(8,128)(2,1)} async-done(((bf16[1024,256]{0,1:T(8,128)(2,1)}), bf16[4096,256]{0,1:T(8,128)(2,1)}) %all-gather.4.cloned.1.call-update) | async-done | bytes 2097168 | tf_op jit(solution)/shard_map/all_gather | solution.py:46
  179.3 3.3 copy.10
  182.5 2.5 broadcast_in_dim.12
  185.0 51.8 %while.14 = (s32[]{:T(128)}, f32[8,256,512]{2,1,0:T(8,128)}, s32[]{:T(128)}, s32[40]{0:T(128)S(1)}, s32[8]{0:T(128)S(1)}, /*index=5*/s32[40]{0:T(128)S(1)}, bf16...) while((s32[]{:T(128)}, f32[8,256,512]{2,1,0:T(8,128)}, ...), condition=%wide.region_8.9_spmd, body=%wide.region_5.8_spmd.sunk | while | flops 134348832 | bytes 2884007 | solution.py:29
  190.1 5.1 conditional.2
  193.1 2.2 fusion.1
  200.3 5.1 conditional.2
  203.3 2.2 fusion.1
  210.6 5.1 conditional.2
  213.5 2.2 fusion.1
  220.8 5.2 conditional.2
  223.8 2.2 fusion.1
  231.0 5.2 conditional.2
  234.0 2.2 fusion.1
  236.9 445.8 %reduce-scatter.2.cloned.1.call-done = f32[1,256,512]{2,1,0:T(8,128)} async-done(((f32[8,256,512]{2,1,0:T(8,128)}), f32[1,256,512]{2,1,0:T(8,128)}) %reduce-scatter.2.cloned.1.call-update) | async-done | bytes 524304 | tf_op jit(solution)/shard_map/reduce_scatter | solution.py:53
  (57 shorter events, 21.5 us)
Async XLA Ops:
  6.5 84.4 %all-gather.6.cloned.1.call-start = ((), (), s32[]{:S(2)}) async-start(), calls=%async_computation.3 | async-start | bytes 8650752 | tf_op jit(solution)/shard_map/all_gather | solution.py:40
  10.6 168.6 %all-gather.4.cloned.1.call-start = ((), (), s32[]{:S(2)}) async-start(), calls=%async_computation.1 | async-start | bytes 2621440 | tf_op jit(solution)/shard_map/all_gather | solution.py:46
  90.9 63.8 %copy-start = (f32[1024,256]{1,0:T(8,128)S(1)}, f32[1024,256]{1,0:T(8,128)}, u32[]{:S(2)}) copy-start(f32[1024,256]{1,0:T(8,128)} %param.10) | copy-start | bytes 3145732
  157.9 524.8 %reduce-scatter.2.cloned.1.call-start = ((), (), s32[]{:S(2)}) async-start(), calls=%async_computation.2 | async-start | bytes 4718592 | tf_op jit(solution)/shard_map/reduce_scatter | solution.py:53
  158.0 27.0 %copy-start.1 = (s32[40]{0:T(128)S(1)}, s32[40]{0:T(128)}, u32[]{:S(2)}) copy-start(s32[40]{0:T(128)} %param.13) | copy-start | bytes 484
  158.0 27.0 %copy-start.2 = (s32[1,8]{1,0:T(1,128)S(1)}, s32[1,8]{1,0:T(1,128)}, u32[]{:S(2)}) copy-start(s32[1,8]{1,0:T(1,128)} %param.15) | copy-start | bytes 100
  158.0 27.0 %copy-start.3 = (s32[40]{0:T(128)S(1)}, s32[40]{0:T(128)}, u32[]{:S(2)}) copy-start(s32[40]{0:T(128)} %param.12) | copy-start | bytes 484
Sparse Core Ops, SparseCore 0:
  10.7 80.1 all-gather.5
  158.1 21.1 all-gather.3
  237.0 445.6 reduce-scatter.1
